TPU v7x, 512 devices: a whole 4x4x16 slice. The times are simulated.
512 devices in a mesh: row: 8 (over z_lo), col: 16 (over x, y), layer: 4 (over z_hi, core).
Axes of the slice: x: 4, y: 4, z: 16 (z_hi: 2, z_lo: 8; z = z_hi * 8 + z_lo), core: 2. Of those that a mesh axis runs over, the one named last changes fastest.
Arguments:
- doubles_amplitude_tensor: float32 [2304, 2048], P('col', 'layer'), may hold values from -6 to 6
- integrals: float32 [8, 16, 4, 96, 2048], P('row', 'col', 'layer'), may hold values from -0.125 to 0.125
- incoming_residual: float32 [2304, 49152], P('col', ('row', 'layer')), may hold values from -6 to 6
Outputs:
- updated_residual: float32 [2304, 49152], P('col', ('row', 'layer'))
All inputs are finite; a program needn't handle non-finite values.
Results may differ from a plain program's by a relative error of at most 0.00005.
Values sent between devices are 32-bit elements; how exact they have to be, the bound alone decides.
No kernel may reach another device: no remote copies, remote signals or barrier semaphores. Data moves between devices by JAX's collectives and lax.ppermute only.
A program may use at most 64 MiB of HBM per device.

v0:
```python
import jax
import jax.numpy as jnp
from jax import lax
from jax.sharding import PartitionSpec as P


def regroup(integrals):
    local = integrals.reshape(1, integrals.shape[3], integrals.shape[4])
    return lax.all_to_all(local, "layer", split_axis=2, concat_axis=0, tiled=True)


def on_device(doubles_amplitude_tensor, integrals, incoming_residual):
    ij_rows = doubles_amplitude_tensor.shape[0]
    regrouped = regroup(integrals)[None]
    partial_ladder_value = jnp.einsum(
        "ic,nlkc->inlk",
        doubles_amplitude_tensor,
        lax.all_gather(regrouped, "col", axis=0, tiled=True),
        precision=lax.Precision.HIGHEST,
        preferred_element_type=jnp.float32,
    )
    summed = lax.psum_scatter(partial_ladder_value, "layer", scatter_dimension=2, tiled=True)
    return incoming_residual + summed.reshape(ij_rows, -1)


def solution(mesh):
    return jax.shard_map(
        on_device,
        mesh=mesh,
        in_specs=(
            P("col", "layer"),
            P("row", "col", "layer", None, None),
            P("col", ("row", "layer")),
        ),
        out_specs=P("col", ("row", "layer")),
        check_vma=False,
    )
```

profile of v0, /device:TPU:1, one launch (start us, length us, event | category | flops | bytes accessed | tf_op | source)
XLA Modules:
  0.0 565.8 jit_solution(12398285052435293716)
XLA Ops:
  6.5 0.0 copy-start
  6.5 0.0 all-gather.3.cloned.1.call-start
  6.5 1.5 copy.7
  8.1 43.3 %all_to_all.15 = f32[1,96,2048]{1,0,2:T(1,128)S(1)} all-to-all(f32[1,96,2048]{1,0,2:T(1,128)S(1)} %bitcast.24), channel_id=1, replica_groups=mesh['row'=8,'col'=16,'layer'=4] {'layer'}, dimensions={2} | all-to-all | bytes 1572864 | tf_op jit(solution)/shard_map/all_to_all | solution.py:9
  51.4 1.2 copy.8
  52.6 0.0 all-gather.3.cloned.1.call-update
  52.6 0.0 all-reduce.3.cloned.1.call-start
  52.6 128.7 %all-gather.3.cloned.1.call-done = f32[64,1,96,512]{3,2,1,0:T(8,128)} async-done(((f32[4,1,96,512]{3,2,1,0:T(8,128)}), f32[64,1,96,512]{3,2,1,0:T(8,128)}) %all-gather.3.cloned.1.call-update) | async-done | bytes 12582928 | tf_op jit(solution)/shard_map/all_gather | solution.py:18
  181.3 0.0 copy-done
  181.4 18.7 %fusion = f32[144,16,4,96]{3,0,2,1:T(8,128)} fusion(f32[144,512]{1,0:T(8,128)S(1)} %copy-done, f32[16,4,96,512]{3,2,1,0:T(8,128)} %bitcast.22), kind=kOutput, calls=%fused_computation | convolution fusion | flops 5435817984 | bytes 16416768 | tf_op jit(solution)/shard_map/ic,nlkc->inlk/dot_general | solution.py:15
  200.1 0.0 copy-start.1
  200.1 0.0 all-reduce.3.cloned.1.call-update
  200.1 1.3 dynamic-slice
  201.5 353.6 %all-reduce.3.cloned.1.call-done = f32[144,16,4,96]{3,0,2,1:T(8,128)} async-done(((f32[144,16,4,96]{3,0,2,1:T(8,128)}), f32[144,16,4,96]{3,0,2,1:T(8,128)}) %all-reduce.3.cloned.1.call-update) | async-done | bytes 3538960
  555.1 2.0 constant_dynamic-slice_fusion
  557.1 0.4 copy.9
  557.5 0.5 reshape.8
  558.0 0.0 copy-done.1
  558.0 1.0 add.5
Async XLA Ops:
  6.5 174.8 %copy-start = (f32[144,512]{1,0:T(8,128)S(1)}, f32[144,512]{1,0:T(8,128)}, u32[]{:S(2)}) copy-start(f32[144,512]{1,0:T(8,128)} %param.3) | copy-start | bytes 884740
  6.5 174.8 %all-gather.3.cloned.1.call-start = ((), (), s32[]{:S(2)}) async-start(), calls=%async_computation.1 | async-start | bytes 13369344 | tf_op jit(solution)/shard_map/all_gather | solution.py:18
  52.6 502.5 %all-reduce.3.cloned.1.call-start = ((), (), s32[]{:S(2)}) async-start(), calls=%async_computation.2 | async-start | bytes 9437184
  200.1 357.9 %copy-start.1 = (f32[144,1536]{1,0:T(8,128)S(1)}, f32[144,1536]{1,0:T(8,128)}, u32[]{:S(2)}) copy-start(f32[144,1536]{1,0:T(8,128)} %param.5) | copy-start | bytes 2654212
Sparse Core Ops, SparseCore 0:
  52.7 128.5 all-gather.2
  200.2 354.7 all-reduce.2
where the time goes:
time: 566 us
  waiting for transfers between devices  482 us (85%)
  blocking collectives  43.3 us (8%)
  matrix products  18.7 us (3%)
  between operations  13.4 us (2%)
  local copies, waits for them, and re-layouts  6.95 us (1%)
    unnamed x3, waiting for transfers between devices  354 us
    all_gather x1, waiting for transfers between devices, on_device(): lax.all_gather(regrouped, 'col', axis=0, tiled=True)  129 us
    all_to_all x1, blocking collectives, regroup(): lax.all_to_all(local, 'layer', split_axis=2, concat_axis=0, tiled=True)  43.3 us
    dot_general x1, matrix products, on_device(): jnp.einsum('ic,nlkc->inlk', doubles_amplitude_tensor, lax.all_gather(regr...  18.7 us
  transfers between devices with their start and end apart: 2, of which 2 were waited for; matrix products, arithmetic and copies ran while one was open for 0% of the time, Pallas kernels for 0%

commit v1 on v0

--- a/solution.py
+++ b/solution.py
@@ -15,7 +15,9 @@
     partial_ladder_value = jnp.einsum(
         "ic,nlkc->inlk",
         doubles_amplitude_tensor,
-        lax.all_gather(regrouped, "col", axis=0, tiled=True),
+        jnp.concatenate(
+            lax.all_to_all(jnp.stack([regrouped] * lax.axis_size("col")), "col", 0, 0), axis=0
+        ),
         precision=lax.Precision.HIGHEST,
         preferred_element_type=jnp.float32,
     )

time: 566 us -> 605 us (1.069)
  blocking collectives: 43.3 us -> 188 us
  waiting for transfers between devices: 482 us -> 377 us
    all_to_all x0 -> x1, blocking collectives: none -> 145 us  [on_device(): lax.all_to_all(jnp.stack([regrouped] * lax.axis_size('col')), 'col', 0, 0)]
    all_gather x1 -> x0, waiting for transfers between devices: 129 us -> none  [on_device(): lax.all_gather(regrouped, 'col', axis=0, tiled=True)]
    unnamed x3 -> x2, waiting for transfers between devices: 354 us -> 377 us
  transfers between devices with their start and end apart: 2 -> 1, of which waited for: 2 -> 1; matrix products, arithmetic and copies ran while one was open for 0% -> 0% of each run, Pallas kernels for 0% -> 0%
where the time goes in v1:
time: 605 us; the launch traced here: 604 us
  waiting for transfers between devices  377 us (62%)
  blocking collectives  188 us (31%)
  matrix products  17.2 us (3%)
  between operations  13.4 us (2%)
  local copies, waits for them, and re-layouts  7.66 us (1%)
    unnamed x2, waiting for transfers between devices  377 us
    all_to_all x1, blocking collectives, on_device(): lax.all_to_all(jnp.stack([regrouped] * lax.axis_size('col')), 'col', 0, 0)  145 us
    all_to_all x1, blocking collectives, regroup(): lax.all_to_all(local, 'layer', split_axis=2, concat_axis=0, tiled=True)  43.3 us
    dot_general x1, matrix products, on_device(): jnp.einsum('ic,nlkc->inlk', doubles_amplitude_tensor, jnp.concatenate(lax...  17.2 us
  transfers between devices with their start and end apart: 1, of which 1 were waited for; matrix products, arithmetic and copies ran while one was open for 0% of the time, Pallas kernels for 0%

profile of v1, /device:TPU:1, one launch (start us, length us, event | category | flops | bytes accessed | tf_op | source)
XLA Modules:
  0.0 604.4 jit_solution(758456448649994578)
XLA Ops:
  6.5 0.0 copy-start
  6.5 0.0 all-reduce.3.cloned.1.call-start
  6.5 1.5 copy.7
  8.1 43.3 %all_to_all.20 = f32[1,96,2048]{1,0,2:T(1,128)S(1)} all-to-all(f32[1,96,2048]{1,0,2:T(1,128)S(1)} %bitcast.24), channel_id=1, replica_groups=mesh['row'=8,'col'=16,'layer'=4] {'layer'}, dimensions={2} | all-to-all | bytes 1572864 | tf_op jit(solution)/shard_map/all_to_all | solution.py:9
  51.4 0.3 copy.8
  51.7 1.6 stack.3
  53.3 144.8 %all_to_all.21 = f32[16,1,4,96,512]{4,3,2,1,0:T(8,128)S(1)} all-to-all(f32[16,1,4,96,512]{4,3,2,1,0:T(8,128)S(1)} %stack.3), channel_id=1, replica_groups=mesh['row'=8,'col'=16,'layer'=4] {'col'}, dimensions={0} | all-to-all | bytes 25165824 | tf_op jit(solution)/shard_map/all_to_all | solution.py:19
  198.1 0.0 copy-done
  198.1 17.2 %fusion = f32[144,16,4,96]{3,0,2,1:T(8,128)} fusion(f32[16,1,4,96,512]{4,3,2,1,0:T(8,128)S(1)} %all_to_all.21, f32[144,512]{1,0:T(8,128)S(1)} %copy-done), kind=kOutput, calls=%fused_computation | convolution fusion | flops 5435817984 | bytes 16416768 | tf_op jit(solution)/shard_map/ic,nlkc->inlk/dot_general | solution.py:15
  215.3 0.0 copy-start.1
  215.3 0.0 all-reduce.3.cloned.1.call-update
  215.3 1.3 dynamic-slice
  216.7 376.9 %all-reduce.3.cloned.1.call-done = f32[144,16,4,96]{3,0,2,1:T(8,128)} async-done(((f32[144,16,4,96]{3,0,2,1:T(8,128)}), f32[144,16,4,96]{3,0,2,1:T(8,128)}) %all-reduce.3.cloned.1.call-update) | async-done | bytes 3538960
  593.6 2.0 constant_dynamic-slice_fusion
  595.6 0.4 copy.9
  596.0 0.5 reshape.16
  596.5 0.0 copy-done.1
  596.5 1.0 add.5
Async XLA Ops:
  6.5 191.5 %copy-start = (f32[144,512]{1,0:T(8,128)S(1)}, f32[144,512]{1,0:T(8,128)}, u32[]{:S(2)}) copy-start(f32[144,512]{1,0:T(8,128)} %param.3) | copy-start | bytes 884740
  6.5 587.1 %all-reduce.3.cloned.1.call-start = ((), (), s32[]{:S(2)}) async-start(), calls=%async_computation.2 | async-start | bytes 9437184
  215.3 381.2 %copy-start.1 = (f32[144,1536]{1,0:T(8,128)S(1)}, f32[144,1536]{1,0:T(8,128)}, u32[]{:S(2)}) copy-start(f32[144,1536]{1,0:T(8,128)} %param.5) | copy-start | bytes 2654212
Sparse Core Ops, SparseCore 0:
  215.4 378.1 all-reduce.2
